TPU v7x, 512 devices: a whole 4x8x8 slice. The times are simulated.
512 devices in a mesh: member: 2 (over core), fsdp: 256 (over y, x, z).
Axes of the slice: x: 4, y: 8, z: 8, core: 2. Of those that a mesh axis runs over, the one named last changes fastest.
Arguments:
- hidden: bfloat16 [2, 512, 2048], P('member', 'fsdp'), may hold values from -60 to 60
- gain: float32 [2, 2048], P('member'), may hold values from 0.5 to 1.5
- head: bfloat16 [2, 2048, 128256], P('member', None, 'fsdp'), may hold values from -0.397747564 to 0.397747564
- labels: int32 [512], replicated, may hold values from 0 to 128255
Outputs:
- token_loss: float32 [2, 512], P('member', 'fsdp')
- head_grad: bfloat16 [2, 2048, 128256], P('member', None, 'fsdp')
- hidden_grad: bfloat16 [2, 512, 2048], P('member', 'fsdp')
All inputs are finite; a program needn't handle non-finite values.
Results may differ from a plain program's by a relative error of at most 0.0049.
Values may be sent and summed in bfloat16 or wider, within the bound.
A program may use at most 64 MiB of HBM per device.

v0:
```python
import jax
import jax.numpy as jnp
from jax import lax
from jax.sharding import PartitionSpec as P

EPS = 1e-05
BETA = 0.5


def swapped(value, axis, bit):
    return lax.ppermute(value, axis, [(i, i ^ 1 << bit) for i in range(lax.axis_size(axis))])


def normalize(rows, gain_row):
    values = rows.astype(jnp.float32)
    inverse = lax.rsqrt(jnp.mean(values * values, axis=-1, keepdims=True) + EPS)
    return ((values * inverse * gain_row).astype(jnp.bfloat16), inverse)


def norm_back(rows, inverse, gain_row, upstream):
    values = rows.astype(jnp.float32)
    scaled = gain_row * upstream
    inner = jnp.mean(scaled * values, axis=-1, keepdims=True)
    return inverse * scaled - values * inverse**3 * inner


def body(hidden, gain, head, labels):
    own_rows = hidden[0]
    gain_row = gain[0]
    weights_local = head[0]
    tok_dev = own_rows.shape[0]
    vocab_dev = weights_local.shape[1]
    own_start = lax.axis_index("fsdp") * tok_dev
    vocab_start = lax.axis_index("fsdp") * vocab_dev
    normed_own, inverse_own = normalize(own_rows, gain_row)
    normed = lax.all_gather(normed_own, "fsdp", axis=0, tiled=True)
    token_count = normed.shape[0]
    logits = jnp.dot(normed, weights_local, preferred_element_type=jnp.float32)
    local_label = labels - vocab_start
    columns = lax.broadcasted_iota(jnp.int32, (1, vocab_dev), 1)
    onehot_mask = local_label[:, None] == columns
    picked_part = jnp.sum(jnp.where(onehot_mask, logits, 0.0), axis=-1)
    row_top = lax.pmax(jnp.max(logits, axis=-1), "fsdp")
    row_total, picked = lax.psum(
        (jnp.sum(jnp.exp(logits - row_top[:, None]), axis=-1), picked_part), "fsdp"
    )
    log_total = row_top + jnp.log(row_total)
    logprob = (logits - log_total[:, None]).astype(jnp.bfloat16)
    teacher = swapped(logprob, "member", 0)
    target = jnp.exp(teacher.astype(jnp.float32))
    student = jnp.exp(logits - log_total[:, None])
    dlogits = (
        ((1.0 + BETA) * student - onehot_mask.astype(jnp.float32) - BETA * target) / token_count
    ).astype(jnp.bfloat16)
    cross_part = jnp.sum(target * (log_total[:, None] - logits), axis=-1)
    head_grad = lax.dot_general(
        normed, dlogits, (((0,), (0,)), ((), ())), preferred_element_type=jnp.float32
    ).astype(jnp.bfloat16)
    cross_whole = lax.psum(cross_part, "fsdp")
    cross_own = lax.dynamic_slice_in_dim(cross_whole, own_start, tok_dev, 0)
    partial_up = lax.dot_general(
        dlogits, weights_local, (((1,), (1,)), ((), ())), preferred_element_type=jnp.float32
    )
    summed = lax.psum_scatter(partial_up, "fsdp", scatter_dimension=0, tiled=True)
    total_own = lax.dynamic_slice_in_dim(log_total, own_start, tok_dev, 0)
    picked_own = lax.dynamic_slice_in_dim(picked, own_start, tok_dev, 0)
    token_loss = total_own - picked_own + BETA * cross_own
    hidden_grad = norm_back(own_rows, inverse_own, gain_row, summed)
    return (token_loss[None], head_grad[None], hidden_grad.astype(jnp.bfloat16)[None])


def solution(mesh):
    in_specs = (P("member", "fsdp", None), P("member", None), P("member", None, "fsdp"), P())
    out_specs = (P("member", "fsdp"), P("member", None, "fsdp"), P("member", "fsdp", None))
    return jax.shard_map(body, mesh=mesh, in_specs=in_specs, out_specs=out_specs, check_vma=False)
```

profile of v0, /device:TPU:32, one launch (start us, length us, event | category | flops | bytes accessed | tf_op | source)
XLA Modules:
  0.0 2223.4 jit_solution(17684733254813426398)
XLA Ops:
  7.2 0.0 copy-start
  7.2 0.0 all-gather.3.cloned.1.call-start
  7.2 1.0 fusion.5
  8.2 1.4 fusion.12
  9.6 0.0 all-gather.3.cloned.1.call-update
  9.6 0.0 all-reduce.4.cloned.1.call-start
  9.7 121.9 %all-gather.3.cloned.1.call-done = bf16[256,2,2048]{2,1,0:T(2,128)(2,1)} async-done(((bf16[1,2,2048]{2,1,0:T(2,128)(2,1)}), bf16[256,2,2048]{2,1,0:T(2,128)(2,1)}) %all-gather.3.cloned.1.call-update) | async-done | bytes 2097168 | tf_op jit(solution)/shard_map/all_gather | solution.py:36
  131.6 4.1 reshape.31
  135.8 0.0 copy-done
  135.8 2.9 fusion.14
  138.6 0.0 copy-start.5
  138.7 688.6 %pmax.7 = f32[512]{0:T(512)S(1)} all-reduce(f32[512]{0:T(512)S(1)} %get-tuple-element.10), channel_id=1, replica_groups=mesh['member'=2,'fsdp'=256] {'fsdp'}, use_global_device_ids=true, to_apply=%region_2.3 | all-reduce | flops 512 | bytes 4096 | tf_op jit(solution)/shard_map/pmax | solution.py:43
  827.3 0.2 exponential_reduce_fusion
  827.5 683.0 %psum.21 = f32[512]{0:T(512)S(1)} all-reduce(f32[512]{0:T(512)S(1)} %exponential_reduce_fusion), channel_id=1, replica_groups=mesh['member'=2,'fsdp'=256] {'fsdp'}, use_global_device_ids=true, to_apply=%region_4.5 | all-reduce | flops 512 | bytes 4096 | tf_op jit(solution)/shard_map/psum | solution.py:44
  1510.5 0.9 subtract_convert_fusion
  1511.4 1.9 collective-permute-start
  1513.3 0.0 copy-done.5
  1513.3 2.2 collective-permute-done
  1515.5 1.7 select_reduce_fusion
  1517.2 0.0 copy-start.1
  1517.2 0.8 copy-done.1
  1518.0 3.3 fusion.1
  1521.3 0.0 copy-start.2
  1521.3 0.0 all-reduce.4.cloned.1.call-update
  1521.3 1.3 dynamic-slice
  1523.3 686.0 %all-reduce.1 = (f32[512]{0:T(512)S(1)}, f32[512]{0:T(512)S(1)}) all-reduce(f32[512]{0:T(512)S(1)} %get-tuple-element.4, f32[512]{0:T(512)S(1)} %get-tuple-element.3), channel_id=1, replica_groups=mesh['member'=2,'fsdp'=256] {'fsdp'}, use_global_device_ids=true, to_apply=%region_8.9 | all-reduce | flops 1024 | bytes 8192 | tf_op jit(solution)/shard_map/psum | solution.py:59
  2209.3 0.6 add_bitcast_fusion
  2209.9 0.0 copy-done.2
  2209.9 0.0 copy-start.3
  2209.9 0.0 copy-start.4
  2209.9 4.2 fusion
  2214.0 0.0 all-reduce.4.cloned.1.call-done
  2214.0 0.0 copy-done.3
  2214.1 0.0 copy-done.4
  2214.1 1.0 fusion.11
  2215.0 1.5 fusion.13
  (4 shorter events, 0.0 us)
Async XLA Ops:
  7.2 128.6 %copy-start = (bf16[1,2048,501]{1,2,0:T(8,128)(2,1)S(1)}, bf16[1,2048,501]{1,2,0:T(8,128)(2,1)}, u32[]{:S(2)}) copy-start(bf16[1,2048,501]{1,2,0:T(8,128)(2,1)} %param.6) | copy-start | bytes 6156292
  7.2 124.4 %all-gather.3.cloned.1.call-start = ((), (), s32[]{:S(2)}) async-start(), calls=%async_computation | async-start | bytes 2105344 | tf_op jit(solution)/shard_map/all_gather | solution.py:36
  9.6 2204.4 %all-reduce.4.cloned.1.call-start = ((), (), s32[]{:S(2)}) async-start(), calls=%async_computation.1 | async-start | bytes 8388608
  138.6 1374.7 %copy-start.5 = (s32[512]{0:T(512)S(1)}, s32[512]{0:T(512)}, u32[]{:S(2)}) copy-start(s32[512]{0:T(512)} %param.7) | copy-start | bytes 6148
  1511.4 4.1 collective-permute-start
  1517.2 0.8 copy-start.1
  1521.3 688.6 %copy-start.2 = (bf16[512,501]{0,1:T(8,128)(2,1)S(1)}, bf16[512,501]{0,1:T(8,128)(2,1)}, u32[]{:S(2)}) copy-start(bf16[512,501]{0,1:T(8,128)(2,1)} %copy-done.1) | copy-start | bytes 1539076
  2209.9 4.2 copy-start.3
  2209.9 4.2 copy-start.4
Sparse Core Ops, SparseCore 0:
  12.6 118.9 all-gather.2
  1521.4 245.9 all-reduce.3
where the time goes:
time: 2220 us
  blocking collectives  2060 us (93%)
  waiting for transfers between devices  124 us (6%)
    pmax x1, blocking collectives, body(): row_top = lax.pmax(jnp.max(logits, axis=-1), 'fsdp')  689 us
    psum x1, blocking collectives, body(): cross_whole = lax.psum(cross_part, 'fsdp')  686 us
    psum x1, blocking collectives, body(): lax.psum((jnp.sum(jnp.exp(logits - row_top[:, None]), axis=-1), picked_pa...  683 us
    all_gather x1, waiting for transfers between devices, body(): normed = lax.all_gather(normed_own, 'fsdp', axis=0, tiled=True)  122 us
  transfers between devices with their start and end apart: 3, of which 2 were waited for; matrix products, arithmetic and copies ran while one was open for 0% of the time, Pallas kernels for 0%

commit v1 on v0

--- a/solution.py
+++ b/solution.py
@@ -56,7 +56,7 @@
     head_grad = lax.dot_general(
         normed, dlogits, (((0,), (0,)), ((), ())), preferred_element_type=jnp.float32
     ).astype(jnp.bfloat16)
-    cross_whole = lax.psum(cross_part, "fsdp")
+    cross_whole = jnp.sum(lax.all_gather(cross_part, "fsdp"), axis=0)
     cross_own = lax.dynamic_slice_in_dim(cross_whole, own_start, tok_dev, 0)
     partial_up = lax.dot_general(
         dlogits, weights_local, (((1,), (1,)), ((), ())), preferred_element_type=jnp.float32

time: 2220 us -> 2900 us (1.31)
  the two profiles are of different devices: /device:TPU:32 before, /device:TPU:64 now
where the time goes in v1:
time: 2900 us
  blocking collectives  2740 us (94%)
  waiting for transfers between devices  125 us (4%)
    psum x2, blocking collectives, body(): lax.psum((jnp.sum(jnp.exp(logits - row_top[:, None]), axis=-1), picked_pa...  1370 us
    pmax x1, blocking collectives, body(): row_top = lax.pmax(jnp.max(logits, axis=-1), 'fsdp')  684 us
    all_gather x1, blocking collectives, body(): cross_whole = jnp.sum(lax.all_gather(cross_part, 'fsdp'), axis=0)  678 us
    all_gather x1, waiting for transfers between devices, body(): normed = lax.all_gather(normed_own, 'fsdp', axis=0, tiled=True)  123 us
  transfers between devices with their start and end apart: 3, of which 2 were waited for; matrix products, arithmetic and copies ran while one was open for 0% of the time, Pallas kernels for 0%

profile of v1, /device:TPU:64, one launch (start us, length us, event | category | flops | bytes accessed | tf_op | source)
XLA Modules:
  0.0 2902.6 jit_solution(10088482010253924896)
XLA Ops:
  7.2 0.0 copy-start
  7.2 0.0 all-gather.5.cloned.1.call-start
  7.2 1.0 fusion.5
  8.2 1.4 fusion.12
  9.6 0.0 all-gather.5.cloned.1.call-update
  9.6 0.0 all-reduce.3.cloned.1.call-start
  9.7 123.2 %all-gather.5.cloned.1.call-done = bf16[256,2,2048]{2,1,0:T(2,128)(2,1)} async-done(((bf16[1,2,2048]{2,1,0:T(2,128)(2,1)}), bf16[256,2,2048]{2,1,0:T(2,128)(2,1)}) %all-gather.5.cloned.1.call-update) | async-done | bytes 2097168 | tf_op jit(solution)/shard_map/all_gather | solution.py:36
  132.8 4.1 reshape.32
  137.0 0.0 copy-done
  137.0 2.9 fusion.14
  139.9 0.0 copy-start.5
  139.9 683.9 %pmax.7 = f32[512]{0:T(512)S(1)} all-reduce(f32[512]{0:T(512)S(1)} %get-tuple-element.8), channel_id=1, replica_groups=mesh['member'=2,'fsdp'=256] {'fsdp'}, use_global_device_ids=true, to_apply=%region_2.3 | all-reduce | flops 512 | bytes 4096 | tf_op jit(solution)/shard_map/pmax | solution.py:43
  823.8 0.2 exponential_reduce_fusion
  823.9 688.2 %psum.14 = f32[512]{0:T(512)S(1)} all-reduce(f32[512]{0:T(512)S(1)} %exponential_reduce_fusion), channel_id=1, replica_groups=mesh['member'=2,'fsdp'=256] {'fsdp'}, use_global_device_ids=true, to_apply=%region_4.5 | all-reduce | flops 512 | bytes 4096 | tf_op jit(solution)/shard_map/psum | solution.py:44
  1512.2 0.9 subtract_convert_fusion
  1513.1 1.9 collective-permute-start
  1515.0 0.0 copy-done.5
  1515.1 2.2 collective-permute-done
  1517.2 1.7 select_reduce_fusion
  1518.9 0.0 copy-start.1
  1519.0 0.8 copy-done.1
  1519.7 3.3 fusion.1
  1523.0 0.0 copy-start.2
  1523.0 0.0 all-reduce.3.cloned.1.call-update
  1523.0 1.3 dynamic-slice
  1525.0 678.1 %all-gather.2 = f32[256,1,512]{2,1,0:T(1,128)S(1)} all-gather(f32[1,1,512]{2,1,0:T(1,128)S(1)} %bitcast.35), channel_id=2, replica_groups=mesh['member'=2,'fsdp'=256] {'fsdp'}, dimensions={0}, use_global_device_ids=true | all-gather | bytes 526336 | tf_op jit(solution)/shard_map/all_gather | solution.py:59
  2203.1 0.3 reduce_sum.58
  2203.4 685.0 %psum.15 = f32[512]{0:T(512)S(1)} all-reduce(f32[512]{0:T(512)S(1)} %get-tuple-element.3), channel_id=1, replica_groups=mesh['member'=2,'fsdp'=256] {'fsdp'}, use_global_device_ids=true, to_apply=%region_6.7 | all-reduce | flops 512 | bytes 4096 | tf_op jit(solution)/shard_map/psum | solution.py:44
  2888.5 0.6 add_bitcast_fusion
  2889.0 0.0 copy-done.2
  2889.0 0.0 copy-start.3
  2889.1 0.0 copy-start.4
  2889.1 4.2 fusion
  2893.2 0.0 all-reduce.3.cloned.1.call-done
  2893.2 0.0 copy-done.3
  2893.2 0.0 copy-done.4
  2893.2 1.0 fusion.11
  2894.2 1.5 fusion.13
  (4 shorter events, 0.0 us)
Async XLA Ops:
  7.2 129.8 %copy-start = (bf16[1,2048,501]{1,2,0:T(8,128)(2,1)S(1)}, bf16[1,2048,501]{1,2,0:T(8,128)(2,1)}, u32[]{:S(2)}) copy-start(bf16[1,2048,501]{1,2,0:T(8,128)(2,1)} %param.6) | copy-start | bytes 6156292
  7.2 125.7 %all-gather.5.cloned.1.call-start = ((), (), s32[]{:S(2)}) async-start(), calls=%async_computation | async-start | bytes 2105344 | tf_op jit(solution)/shard_map/all_gather | solution.py:36
  9.6 2883.6 %all-reduce.3.cloned.1.call-start = ((), (), s32[]{:S(2)}) async-start(), calls=%async_computation.1 | async-start | bytes 8388608
  139.9 1375.2 %copy-start.5 = (s32[512]{0:T(512)S(1)}, s32[512]{0:T(512)}, u32[]{:S(2)}) copy-start(s32[512]{0:T(512)} %param.7) | copy-start | bytes 6148
  1513.1 4.1 collective-permute-start
  1518.9 0.8 copy-start.1
  1523.0 1366.0 %copy-start.2 = (bf16[512,501]{0,1:T(8,128)(2,1)S(1)}, bf16[512,501]{0,1:T(8,128)(2,1)}, u32[]{:S(2)}) copy-start(bf16[512,501]{0,1:T(8,128)(2,1)} %copy-done.1) | copy-start | bytes 1539076
  2889.0 4.2 copy-start.3
  2889.1 4.2 copy-start.4
Sparse Core Ops, SparseCore 0:
  12.6 120.1 all-gather.4
  1523.2 244.8 all-reduce.2
